TPU v7x, 32 devices: a whole 2x2x4 slice. The times are simulated.
32 devices in a mesh: rep: 4 (over x, core), stripe: 8 (over z, y).
Axes of the slice: x: 2, y: 2, z: 4, core: 2. Of those that a mesh axis runs over, the one named last changes fastest.
Arguments:
- activations: bfloat16 [1024, 1024], P('rep'), may hold values from -6 to 6
- out_grads: bfloat16 [1024, 4096], P('rep', 'stripe'), may hold values from -4 to 4
- statistics: float32 [4, 8, 512, 512], P('rep', 'stripe'), may hold values from -48 to 4608, as said below
- owner_blocks: int32 [8, 2], P('stripe'), may hold values from 0 to 1, each once within a row
Outputs:
- preconditioned: float32 [1024, 4096], P(None, 'stripe')
- new_stats: float32 [4, 8, 512, 512], P('rep', 'stripe')
Inputs may be any that keep to these rules, and one draw needn't show every extreme that they name: statistics[p, s] is symmetric positive definite for every p and s. `owner_blocks`: each row lists every row block 0 to 1 exactly once.
All inputs are finite; a program needn't handle non-finite values.
Results may differ from a plain program's by a relative error of at most 0.0003.
Values sent between devices are 32-bit elements; how exact they have to be, the bound alone decides.
No kernel may reach another device: no remote copies, remote signals or barrier semaphores. Data moves between devices by JAX's collectives and lax.ppermute only.
A program may use at most 128 MiB of HBM per device.

v0:
```python
import jax
import jax.numpy as jnp
from jax import lax
from jax.sharding import PartitionSpec as P

BLOCK = 512
ITERS = 2
decay_rate = 0.95
damping = 0.25
epsilon = 1e-06
highest = lax.Precision.HIGHEST


def partner(shard, axis, stride):
    return lax.ppermute(shard, axis, [(i, i ^ 1 << stride) for i in range(lax.axis_size(axis))])


def inverse_root(damped):
    identity = jnp.eye(damped.shape[-1], dtype=damped.dtype)
    frob_norm = jnp.sqrt(jnp.sum(damped * damped, axis=(-2, -1), keepdims=True) + epsilon)
    scaled = damped / frob_norm
    root_now = identity * frob_norm ** (-0.25)
    for sweep in range(ITERS):
        factor = (5.0 * identity - scaled) * 0.25
        root_now = jnp.matmul(root_now, factor, precision=highest)
        if sweep + 1 < ITERS:
            square = jnp.matmul(factor, factor, precision=highest)
            fourth = jnp.matmul(square, square, precision=highest)
            scaled = jnp.matmul(fourth, scaled, precision=highest)
    return root_now


def slot_terms(activations, out_grads, blocks_of, pair_count, piece_rows, row_count):
    tokens_here, in_width = activations.shape
    per_block = BLOCK // piece_rows
    shaped = activations.reshape(tokens_here, in_width // piece_rows, piece_rows)
    slot_count = row_count // piece_rows
    slot_ids = jnp.arange(slot_count, dtype=jnp.int32)
    block_ids = jnp.take(blocks_of, slot_ids % pair_count)
    half_ids = slot_ids // pair_count % per_block
    chosen = jnp.take(shaped, block_ids * per_block + half_ids, axis=1)
    products = jnp.einsum("tkp,tc->kpc", chosen, out_grads, preferred_element_type=jnp.float32)
    return products.reshape(slot_count * piece_rows, out_grads.shape[1])


def per_device(activations, out_grads, statistics, owner_blocks):
    rep_count = lax.axis_size("rep")
    pair_count = rep_count // 2
    pair_bit = rep_count.bit_length() - 2
    half_rows = BLOCK // 2
    my_index = lax.axis_index("rep")
    is_left = my_index < pair_count
    blocks_of = owner_blocks[0]
    own_half = lax.psum_scatter(
        slot_terms(
            activations,
            out_grads,
            blocks_of,
            pair_count,
            half_rows,
            half_rows * lax.axis_size("rep"),
        ),
        "rep",
        scatter_dimension=0,
        tiled=True,
    )
    partner_half = partner(own_half, "rep", pair_bit)
    gradient = jnp.where(
        is_left,
        jnp.concatenate([own_half, partner_half], axis=0),
        jnp.concatenate([partner_half, own_half], axis=0),
    )
    facing = jnp.where(is_left, gradient, gradient.T)
    new_stat = decay_rate * statistics[0, 0] + jnp.dot(facing, facing.T, precision=highest)
    trace_sum = lax.psum(jnp.trace(new_stat), ("rep", "stripe"))
    mean_diag = trace_sum / (rep_count * lax.axis_size("stripe") * BLOCK)
    identity = jnp.eye(BLOCK, dtype=jnp.float32)
    root_now = inverse_root(new_stat + damping * mean_diag * identity)
    partner_root = partner(root_now, "rep", pair_bit)
    left_root = jnp.where(is_left, root_now, partner_root)
    right_root = jnp.where(is_left, partner_root, root_now)
    row_start = jnp.where(is_left, 0, half_rows).astype(jnp.int32)
    my_rows = lax.dynamic_slice_in_dim(left_root, row_start, half_rows, 0)
    grad_rows = lax.dynamic_slice_in_dim(gradient, row_start, half_rows, 0)
    precond_half = jnp.dot(
        jnp.dot(my_rows, gradient, precision=highest), right_root, precision=highest
    )
    grad_sq, prec_sq = lax.psum(
        (jnp.sum(grad_rows * grad_rows), jnp.sum(precond_half * precond_half)), ("rep", "stripe")
    )
    scaled = precond_half * jnp.sqrt(grad_sq / (prec_sq + epsilon))
    gathered = lax.all_gather(scaled[None], "rep", axis=0, tiled=True)
    pair_ids = jnp.arange(pair_count, dtype=jnp.int32)
    inverse = jnp.sum(
        pair_ids[:, None] * (blocks_of[:, None] == pair_ids[None, :]).astype(jnp.int32), axis=0
    )
    row_order = jnp.stack([inverse, inverse + pair_count], axis=1).reshape(-1)
    preconditioned = jnp.take(gathered, row_order, axis=0).reshape(
        pair_count * BLOCK, gathered.shape[2]
    )
    return (preconditioned, new_stat[None, None])


def solution(mesh):
    in_specs = (
        P("rep", None),
        P("rep", "stripe"),
        P("rep", "stripe", None, None),
        P("stripe", None),
    )
    out_specs = (P(None, "stripe"), P("rep", "stripe", None, None))
    return jax.shard_map(
        per_device, mesh=mesh, in_specs=in_specs, out_specs=out_specs, check_vma=False
    )
```

profile of v0, /device:TPU:0, one launch (start us, length us, event | category | flops | bytes accessed | tf_op | source)
XLA Modules:
  0.0 226.6 jit_solution(13297253253330376592)
XLA Ops:
  7.2 0.0 copy-start
  7.2 0.0 reduce-scatter.2.cloned.1.call-start
  7.2 0.8 fusion.28
  8.0 0.1 copy.25
  8.1 0.1 reshape.203
  8.2 1.3 gather_fusion
  9.6 1.2 copy.26
  10.8 0.2 copy.27
  11.0 0.6 gather_fusion.1
  11.6 0.0 copy-done
  11.6 0.6 fusion.12
  12.2 1.8 copy.29
  14.0 0.0 reduce-scatter.2.cloned.1.call-update
  14.0 0.0 all-gather.3.cloned.1.call-start
  14.1 34.0 %reduce-scatter.2.cloned.1.call-done = f32[256,512]{0,1:T(8,128)} async-done(((f32[1024,512]{0,1:T(8,128)}), f32[256,512]{0,1:T(8,128)}) %reduce-scatter.2.cloned.1.call-update) | async-done | bytes 524304 | tf_op jit(solution)/shard_map/reduce_scatter | solution.py:54
  48.1 0.4 collective-permute-start
  48.5 13.4 %collective-permute-done = f32[256,512]{0,1:T(8,128)S(1)} collective-permute-done((f32[256,512]{0,1:T(8,128)}, f32[256,512]{0,1:T(8,128)S(1)}, u32[]{:S(2)}, u32[]{:S(2)}) %collective-permute-start) | collective-permute-done | bytes 524320 | tf_op jit(solution)/shard_map/ppermute | solution.py:15
  61.8 0.0 copy-start.2
  61.8 1.6 maximum_select_fusion
  63.4 0.0 copy-done.2
  63.4 0.3 copy.31
  63.8 5.6 %select_reduce_fusion = (f32[]{:T(128)}, f32[512,512]{1,0:T(8,128)S(1)}) fusion(f32[512,512]{1,0:T(8,128)S(1)} %copy.31, pred[]{:T(512)S(6)} %lt.75, f32[256,512]{0,1:T(8,128)} %reduce-scatter.2.cloned.1.call-done, f32[256,512]{0,1:T(8,128)} %copy-done.2, f32[1,1,512,512]{3,2,1,0:T(8,128)} %param.6), kind=kOutput, calls=%fused_computation.17 | convolution fusion | flops 1612972032 | bytes 4194309 | tf_op jit(solution)/shard_map/dot_general | solution.py:74
  69.4 0.0 copy-start.1
  69.4 39.7 %psum.21 = f32[]{:T(128)} all-reduce(f32[]{:T(128)} %get-tuple-element.4), channel_id=1, replica_groups=mesh['rep'=4,'stripe'=8] {'rep','stripe'}, use_global_device_ids=true, to_apply=%region_3.4 | all-reduce | flops 1 | bytes 8 | tf_op jit(solution)/shard_map/psum | solution.py:75
  109.6 1.0 multiply_reduce_fusion
  111.3 2.0 fusion.7
  113.4 1.9 fusion.4
  115.3 1.8 fusion.47
  117.2 0.0 copy-done.1
  117.2 1.9 fusion
  119.1 1.9 fusion.48
  121.0 2.3 %collective-permute-start.1 = (f32[512,512]{1,0:T(8,128)S(1)}, f32[512,512]{1,0:T(8,128)S(1)}, u32[]{:S(2)}, u32[]{:S(2)}) collective-permute-start(f32[512,512]{1,0:T(8,128)S(1)} %fusion.48), channel_id=1, source_target_pairs={{0,16},{8,24},{16,0},{24,8},{1,17},{9,25},{17,1},{25,9},{2,18},{10... | collective-permute-start | bytes 3145736 | tf_op jit(solution)/shard_map/ppermute | solution.py:15
  123.3 0.8 multiply_reduce_fusion.2
  124.1 21.7 %collective-permute-done.1 = f32[512,512]{1,0:T(8,128)S(1)} collective-permute-done((f32[512,512]{1,0:T(8,128)S(1)}, f32[512,512]{1,0:T(8,128)S(1)}, u32[]{:S(2)}, u32[]{:S(2)}) %collective-permute-start.1) | collective-permute-done | bytes 1048608 | tf_op jit(solution)/shard_map/ppermute | solution.py:15
  145.8 2.7 %fusion.10 = f32[256,512]{1,0:T(8,128)S(1)} fusion(f32[512,512]{1,0:T(8,128)S(1)} %collective-permute-done.1, s32[]{:T(128)S(6)} %select_n.184, f32[512,512]{1,0:T(8,128)S(1)} %fusion.48, pred[]{:T(512)S(6)} %lt.75, f32[256,512]{0,1:T(8,128)} %copy-done.2, f32[256,512]{0,1:T(8,128)} %reduce-scatter.2.cloned.1.call-done), kind=kOutput, calls=%fused_computation.22 | convolution fusion | flops 806223872 | bytes 2622976 | tf_op jit(solution)/shard_map/dot_general | solution.py:86
  148.5 1.8 multiply_reduce_fusion.1
  150.3 39.7 %all-reduce = (f32[]{:T(128)}, f32[]{:T(128)}) all-reduce(f32[]{:T(128)} %multiply_reduce_fusion.2, f32[]{:T(128)} %get-tuple-element.6), channel_id=1, replica_groups=mesh['rep'=4,'stripe'=8] {'rep','stripe'}, use_global_device_ids=true, to_apply=%region_6.7 | all-reduce | flops 2 | bytes 16 | tf_op jit(solution)/shard_map/psum | solution.py:88
  191.4 0.8 broadcast_multiply_fusion
  192.2 0.0 all-gather.3.cloned.1.call-update
  192.2 0.1 reshape.206
  192.3 0.1 broadcast_in_dim.39
  192.4 23.6 %all-gather.3.cloned.1.call-done = f32[1024,512]{1,0:T(8,128)} async-done(((f32[256,512]{1,0:T(8,128)}), f32[1024,512]{1,0:T(8,128)}) %all-gather.3.cloned.1.call-update) | async-done | bytes 2097168 | tf_op jit(solution)/shard_map/all_gather | solution.py:92
  216.0 2.3 %gather_fusion.2 = f32[4,256,512]{2,1,0:T(8,128)S(1)} fusion(f32[4,256,512]{2,1,0:T(8,128)} %bitcast.41, s32[1024]{0:T(1024)S(1)} %pad_clamp_fusion), kind=kCustom, calls=%fused_computation.2 | custom fusion | bytes 4194320 | tf_op jit(solution)/shard_map/jit(_take)/gather | solution.py:98
  218.2 1.5 bitcast_select_fusion
  (10 shorter events, 0.1 us)
Async XLA Ops:
  7.2 4.4 %copy-start = (bf16[256,512]{1,0:T(8,128)(2,1)S(1)}, bf16[256,512]{1,0:T(8,128)(2,1)}, u32[]{:S(2)}) copy-start(bf16[256,512]{1,0:T(8,128)(2,1)} %param.5) | copy-start | bytes 786436
  7.2 40.9 %reduce-scatter.2.cloned.1.call-start = ((), (), s32[]{:S(2)}) async-start(), calls=%async_computation.1 | async-start | bytes 2621440 | tf_op jit(solution)/shard_map/reduce_scatter | solution.py:54
  14.0 201.9 %all-gather.3.cloned.1.call-start = ((), (), s32[]{:S(2)}) async-start(), calls=%async_computation.2 | async-start | bytes 2621440 | tf_op jit(solution)/shard_map/all_gather | solution.py:92
  48.1 13.7 %collective-permute-start = (f32[256,512]{0,1:T(8,128)}, f32[256,512]{0,1:T(8,128)S(1)}, u32[]{:S(2)}, u32[]{:S(2)}) collective-permute-start(f32[256,512]{0,1:T(8,128)} %reduce-scatter.2.cloned.1.call-done), channel_id=1, source_target_pairs={{0,16},{8,24},{16,0},{24,8},{1,17},{9,25},{17,1},{25,9},{2,18},{10... | collective-permute-start | bytes 1572872 | tf_op jit(solution)/shard_map/ppermute | solution.py:15
  61.8 1.6 copy-start.2
  69.4 47.8 %copy-start.1 = (f32[512,512]{1,0:T(8,128)}, f32[512,512]{1,0:T(8,128)S(1)}, u32[]{:S(2)}) copy-start(f32[512,512]{1,0:T(8,128)S(1)} %get-tuple-element.5) | copy-start | bytes 3145732
  121.0 24.9 %collective-permute-start.1 = (f32[512,512]{1,0:T(8,128)S(1)}, f32[512,512]{1,0:T(8,128)S(1)}, u32[]{:S(2)}, u32[]{:S(2)}) collective-permute-start(f32[512,512]{1,0:T(8,128)S(1)} %fusion.48), channel_id=1, source_target_pairs={{0,16},{8,24},{16,0},{24,8},{1,17},{9,25},{17,1},{25,9},{2,18},{10... | collective-permute-start | bytes 3145736 | tf_op jit(solution)/shard_map/ppermute | solution.py:15
Sparse Core Ops, SparseCore 0:
  14.2 33.8 reduce-scatter.1
  192.3 23.5 all-gather.2
where the time goes:
time: 227 us
  waiting for transfers between devices  92.7 us (41%)
  blocking collectives  79.4 us (35%)
  matrix products  20.2 us (9%)
  between operations  16.9 us (7%)
  local copies, waits for them, and re-layouts  8.1 us (4%)
  other arithmetic  6.57 us (3%)
  starting transfers between devices  2.79 us (1%)
    psum x1, blocking collectives, per_device(): lax.psum((jnp.sum(grad_rows * grad_rows), jnp.sum(precond_half * precond_...  39.7 us
    psum x1, blocking collectives, per_device(): trace_sum = lax.psum(jnp.trace(new_stat), ('rep', 'stripe'))  39.7 us
    ppermute x2, waiting for transfers between devices, partner(): lax.ppermute(shard, axis, [(i, i ^ 1 << stride) for i in range(lax.axis_s...  35.1 us
    reduce_scatter x1, waiting for transfers between devices, per_device(): lax.psum_scatter(slot_terms(activations, out_grads, blocks_of, pair_count...  34 us
    all_gather x1, waiting for transfers between devices, per_device(): gathered = lax.all_gather(scaled[None], 'rep', axis=0, tiled=True)  23.6 us
    dot_general x1, matrix products, per_device(): jnp.dot(facing, facing.T, precision=highest)  5.62 us
  transfers between devices with their start and end apart: 4, of which 4 were waited for; matrix products, arithmetic and copies ran while one was open for 0% of the time, Pallas kernels for 0%

commit v1 on v0

--- a/solution.py
+++ b/solution.py
@@ -72,7 +72,7 @@
     )
     facing = jnp.where(is_left, gradient, gradient.T)
     new_stat = decay_rate * statistics[0, 0] + jnp.dot(facing, facing.T, precision=highest)
-    trace_sum = lax.psum(jnp.trace(new_stat), ("rep", "stripe"))
+    trace_sum = jnp.sum(lax.all_gather(jnp.trace(new_stat), ("rep", "stripe")), axis=0)
     mean_diag = trace_sum / (rep_count * lax.axis_size("stripe") * BLOCK)
     identity = jnp.eye(BLOCK, dtype=jnp.float32)
     root_now = inverse_root(new_stat + damping * mean_diag * identity)

time: 227 us -> 228 us (level)
    psum x1 -> x0, blocking collectives: 39.7 us -> none  [per_device(): trace_sum = lax.psum(jnp.trace(new_stat), ('rep', 'stripe'))]
    unnamed x0 -> x1, blocking collectives: none -> 39.4 us
where the time goes in v1:
time: 228 us
  waiting for transfers between devices  92.4 us (41%)
  blocking collectives  79.2 us (35%)
  matrix products  20.2 us (9%)
  between operations  17.1 us (8%)
  local copies, waits for them, and re-layouts  8.9 us (4%)
  other arithmetic  7.25 us (3%)
  starting transfers between devices  2.78 us (1%)
    psum x1, blocking collectives, per_device(): lax.psum((jnp.sum(grad_rows * grad_rows), jnp.sum(precond_half * precond_...  39.7 us
    unnamed x1, blocking collectives  39.4 us
    ppermute x2, waiting for transfers between devices, partner(): lax.ppermute(shard, axis, [(i, i ^ 1 << stride) for i in range(lax.axis_s...  34.9 us
    reduce_scatter x1, waiting for transfers between devices, per_device(): lax.psum_scatter(slot_terms(activations, out_grads, blocks_of, pair_count...  34 us
    all_gather x1, waiting for transfers between devices, per_device(): gathered = lax.all_gather(scaled[None], 'rep', axis=0, tiled=True)  23.5 us
    dot_general x1, matrix products, per_device(): jnp.dot(facing, facing.T, precision=highest)  5.62 us
  transfers between devices with their start and end apart: 4, of which 4 were waited for; matrix products, arithmetic and copies ran while one was open for 0% of the time, Pallas kernels for 0%

profile of v1, /device:TPU:0, one launch (start us, length us, event | category | flops | bytes accessed | tf_op | source)
XLA Modules:
  0.0 227.8 jit_solution(12759143974033136031)
XLA Ops:
  7.2 0.0 copy-start
  7.2 0.0 reduce-scatter.2.cloned.1.call-start
  7.2 0.8 fusion.28
  8.0 0.1 copy.25
  8.1 0.1 reshape.203
  8.2 1.3 gather_fusion
  9.6 1.2 copy.26
  10.8 0.2 copy.27
  11.0 0.6 gather_fusion.1
  11.6 0.0 copy-done
  11.6 0.6 fusion.12
  12.2 1.8 copy.29
  14.0 0.0 reduce-scatter.2.cloned.1.call-update
  14.0 0.0 all-gather.3.cloned.1.call-start
  14.1 34.0 %reduce-scatter.2.cloned.1.call-done = f32[256,512]{0,1:T(8,128)} async-done(((f32[1024,512]{0,1:T(8,128)}), f32[256,512]{0,1:T(8,128)}) %reduce-scatter.2.cloned.1.call-update) | async-done | bytes 524304 | tf_op jit(solution)/shard_map/reduce_scatter | solution.py:54
  48.1 0.4 collective-permute-start
  48.5 13.4 %collective-permute-done = f32[256,512]{0,1:T(8,128)S(1)} collective-permute-done((f32[256,512]{0,1:T(8,128)}, f32[256,512]{0,1:T(8,128)S(1)}, u32[]{:S(2)}, u32[]{:S(2)}) %collective-permute-start) | collective-permute-done | bytes 524320 | tf_op jit(solution)/shard_map/ppermute | solution.py:15
  61.8 0.0 copy-start.2
  61.8 1.6 maximum_select_fusion
  63.4 0.0 copy-done.2
  63.4 0.3 copy.31
  63.8 5.6 %select_reduce_fusion = (f32[]{:T(128)}, f32[512,512]{1,0:T(8,128)S(1)}) fusion(f32[512,512]{1,0:T(8,128)S(1)} %copy.31, pred[]{:T(512)S(6)} %lt.75, f32[256,512]{0,1:T(8,128)} %reduce-scatter.2.cloned.1.call-done, f32[256,512]{0,1:T(8,128)} %copy-done.2, f32[1,1,512,512]{3,2,1,0:T(8,128)} %param.6), kind=kOutput, calls=%fused_computation.17 | convolution fusion | flops 1612972032 | bytes 4194309 | tf_op jit(solution)/shard_map/dot_general | solution.py:74
  69.4 0.0 copy-start.1
  69.4 0.8 dynamic-update-slice
  70.2 39.4 %all-reduce = f32[32]{0:T(128)S(1)} all-reduce(f32[32]{0:T(128)S(1)} %dynamic-update-slice), channel_id=1, replica_groups=mesh['rep'=4,'stripe'=8] {'rep','stripe'}, use_global_device_ids=true, to_apply=%add | all-reduce | flops 32 | bytes 256
  109.6 0.7 reduce_sum.57
  111.0 1.0 multiply_reduce_fusion
  112.7 2.0 fusion.7
  114.7 1.9 fusion.4
  116.7 1.8 fusion.47
  118.5 0.0 copy-done.1
  118.5 1.9 fusion
  120.4 1.9 fusion.48
  122.3 2.3 %collective-permute-start.1 = (f32[512,512]{1,0:T(8,128)S(1)}, f32[512,512]{1,0:T(8,128)S(1)}, u32[]{:S(2)}, u32[]{:S(2)}) collective-permute-start(f32[512,512]{1,0:T(8,128)S(1)} %fusion.48), channel_id=1, source_target_pairs={{0,16},{8,24},{16,0},{24,8},{1,17},{9,25},{17,1},{25,9},{2,18},{10... | collective-permute-start | bytes 3145736 | tf_op jit(solution)/shard_map/ppermute | solution.py:15
  124.6 0.8 multiply_reduce_fusion.2
  125.5 21.5 %collective-permute-done.1 = f32[512,512]{1,0:T(8,128)S(1)} collective-permute-done((f32[512,512]{1,0:T(8,128)S(1)}, f32[512,512]{1,0:T(8,128)S(1)}, u32[]{:S(2)}, u32[]{:S(2)}) %collective-permute-start.1) | collective-permute-done | bytes 1048608 | tf_op jit(solution)/shard_map/ppermute | solution.py:15
  147.0 2.7 %fusion.10 = f32[256,512]{1,0:T(8,128)S(1)} fusion(f32[512,512]{1,0:T(8,128)S(1)} %collective-permute-done.1, s32[]{:T(128)S(6)} %select_n.184, f32[512,512]{1,0:T(8,128)S(1)} %fusion.48, pred[]{:T(512)S(6)} %lt.75, f32[256,512]{0,1:T(8,128)} %copy-done.2, f32[256,512]{0,1:T(8,128)} %reduce-scatter.2.cloned.1.call-done), kind=kOutput, calls=%fused_computation.22 | convolution fusion | flops 806223872 | bytes 2622976 | tf_op jit(solution)/shard_map/dot_general | solution.py:86
  149.7 1.8 multiply_reduce_fusion.1
  151.4 39.7 %all-reduce.1 = (f32[]{:T(128)}, f32[]{:T(128)}) all-reduce(f32[]{:T(128)} %multiply_reduce_fusion.2, f32[]{:T(128)} %get-tuple-element.6), channel_id=1, replica_groups=mesh['rep'=4,'stripe'=8] {'rep','stripe'}, use_global_device_ids=true, to_apply=%region_6.7 | all-reduce | flops 2 | bytes 16 | tf_op jit(solution)/shard_map/psum | solution.py:88
  192.5 0.8 broadcast_multiply_fusion
  193.4 0.0 all-gather.3.cloned.1.call-update
  193.4 0.1 reshape.206
  193.5 0.1 broadcast_in_dim.39
  193.6 23.5 %all-gather.3.cloned.1.call-done = f32[1024,512]{1,0:T(8,128)} async-done(((f32[256,512]{1,0:T(8,128)}), f32[1024,512]{1,0:T(8,128)}) %all-gather.3.cloned.1.call-update) | async-done | bytes 2097168 | tf_op jit(solution)/shard_map/all_gather | solution.py:92
  217.1 2.3 gather_fusion.2
  219.4 1.5 bitcast_select_fusion
  (11 shorter events, 0.1 us)
Async XLA Ops:
  7.2 4.4 %copy-start = (bf16[256,512]{1,0:T(8,128)(2,1)S(1)}, bf16[256,512]{1,0:T(8,128)(2,1)}, u32[]{:S(2)}) copy-start(bf16[256,512]{1,0:T(8,128)(2,1)} %param.5) | copy-start | bytes 786436
  7.2 40.9 %reduce-scatter.2.cloned.1.call-start = ((), (), s32[]{:S(2)}) async-start(), calls=%async_computation.1 | async-start | bytes 2621440 | tf_op jit(solution)/shard_map/reduce_scatter | solution.py:54
  14.0 203.1 %all-gather.3.cloned.1.call-start = ((), (), s32[]{:S(2)}) async-start(), calls=%async_computation.2 | async-start | bytes 2621440 | tf_op jit(solution)/shard_map/all_gather | solution.py:92
  48.1 13.7 %collective-permute-start = (f32[256,512]{0,1:T(8,128)}, f32[256,512]{0,1:T(8,128)S(1)}, u32[]{:S(2)}, u32[]{:S(2)}) collective-permute-start(f32[256,512]{0,1:T(8,128)} %reduce-scatter.2.cloned.1.call-done), channel_id=1, source_target_pairs={{0,16},{8,24},{16,0},{24,8},{1,17},{9,25},{17,1},{25,9},{2,18},{10... | collective-permute-start | bytes 1572872 | tf_op jit(solution)/shard_map/ppermute | solution.py:15
  61.8 1.6 copy-start.2
  69.4 49.1 %copy-start.1 = (f32[512,512]{1,0:T(8,128)}, f32[512,512]{1,0:T(8,128)S(1)}, u32[]{:S(2)}) copy-start(f32[512,512]{1,0:T(8,128)S(1)} %get-tuple-element.5) | copy-start | bytes 3145732
  122.3 24.7 %collective-permute-start.1 = (f32[512,512]{1,0:T(8,128)S(1)}, f32[512,512]{1,0:T(8,128)S(1)}, u32[]{:S(2)}, u32[]{:S(2)}) collective-permute-start(f32[512,512]{1,0:T(8,128)S(1)} %fusion.48), channel_id=1, source_target_pairs={{0,16},{8,24},{16,0},{24,8},{1,17},{9,25},{17,1},{25,9},{2,18},{10... | collective-permute-start | bytes 3145736 | tf_op jit(solution)/shard_map/ppermute | solution.py:15
Sparse Core Ops, SparseCore 0:
  14.2 33.8 reduce-scatter.1
  193.5 23.5 all-gather.2
